TPU v7x, 128 devices: a whole 4x4x4 slice. The times are simulated.
128 devices in a mesh: wide: 16 (over y, x), narrow: 8 (over z, core).
Axes of the slice: x: 4, y: 4, z: 4, core: 2. Of those that a mesh axis runs over, the one named last changes fastest.
Arguments:
- diag_block: float32 [256, 256], P('narrow'), as said below
- panel_below: float32 [24576, 256], P(('wide', 'narrow')), may hold values from -0.216 to 0.216
- trailing_slab: float32 [12288, 24576], P('narrow', 'wide'), may hold values from -6 to 6
Outputs:
- updated: float32 [12288, 24576], P('narrow', 'wide')
Inputs may be any that keep to these rules, and one draw needn't show every extreme that they name: `diag_block`: symmetric positive definite; its smallest eigenvalue is 0.01 or more and its diagonal entries lie between 0.4 and 2.1.
All inputs are finite; a program needn't handle non-finite values.
Results may differ from a plain program's by a relative error of at most 0.00016.
Values sent between devices are 32-bit elements; how exact they have to be, the bound alone decides.
A program may use at most 64 MiB of HBM per device.

v0:
```python
import jax
import jax.numpy as jnp
from jax import lax
from jax.sharding import PartitionSpec as P

unit_gamma = 65538.0 * 2.0 ** (-24) / (1.0 - 65538.0 * 2.0 ** (-24))


def from_root(block, axis, source):
    block = jnp.where(lax.axis_index(axis) == source, block, jnp.zeros_like(block))
    return lax.psum(block, axis)


def factor_block(diag_full):
    trace_sum = jnp.sum(jnp.diagonal(diag_full))
    shift_value = unit_gamma * trace_sum / diag_full.shape[0]
    identity = jnp.eye(diag_full.shape[0], dtype=jnp.float32)
    return jnp.linalg.cholesky(diag_full - shift_value * identity)


def solve_rows(raw_panel, lower_factor):
    return jax.scipy.linalg.solve_triangular(lower_factor, raw_panel.T, lower=True).T


def on_device(diag_block, panel_below, trailing_slab):
    diag_full = lax.all_gather(diag_block, "narrow", axis=0, tiled=True)
    lower_factor = factor_block(diag_full)
    owner = lax.axis_index("narrow")
    solved_mine = solve_rows(panel_below, lower_factor)
    column_panel = lax.all_gather(solved_mine, "narrow", axis=0, tiled=True)
    row_panel = from_root(column_panel, "wide", owner)
    product = lax.dot_general(
        row_panel,
        column_panel,
        (((1,), (1,)), ((), ())),
        precision=lax.Precision.HIGHEST,
        preferred_element_type=jnp.float32,
    )
    return trailing_slab - product


def solution(mesh):
    placed = (P("narrow", None), P(("wide", "narrow"), None), P("narrow", "wide"))
    return jax.shard_map(
        on_device, mesh=mesh, in_specs=placed, out_specs=P("narrow", "wide"), check_vma=False
    )
```

profile of v0, /device:TPU:0, one launch (start us, length us, event | category | flops | bytes accessed | tf_op | source)
XLA Modules:
  0.0 223.8 jit_solution(3834586539519067064)
XLA Ops:
  6.5 0.0 all-gather.2.cloned.1.call-start
  6.6 14.3 %all_gather.6 = f32[256,256]{1,0:T(8,128)S(1)} all-gather(f32[32,256]{1,0:T(8,128)} %param.3), channel_id=1, replica_groups=mesh['wide'=16,'narrow'=8] {'narrow'}, dimensions={0}, use_global_device_ids=true | all-gather | bytes 294912 | tf_op jit(solution)/shard_map/all_gather | solution.py:26
  20.9 0.1 copy.23
  21.0 2.3 %gather_fusion = f32[256]{0:T(256)S(1)} fusion(f32[256,256]{1,0:T(8,128)S(1)} %all_gather.6, s32[256]{0:T(256)S(1)} %bitcast.35), kind=kCustom, calls=%fused_computation | custom fusion | bytes 4096 | tf_op jit(solution)/shard_map/jit(diagonal)/cond/branch_0_fun/gather | solution.py:15
  23.4 0.6 reduce_sum.9
  24.7 0.1 copy.24
  24.9 11.7 %cholesky.49 = f32[128,128]{1,0:T(8,128)S(1)} custom-call(f32[128,128]{1,0:T(8,128)S(1)} %cholesky.115), custom_call_target="Cholesky" | custom-call | tf_op jit(solution)/shard_map/jit(cholesky)/cholesky | solution.py:18
  36.6 0.1 copy.25
  36.7 9.8 %custom-call.15 = f32[1,128,128]{1,2,0:T(8,128)S(1)} custom-call(f32[1,128,128]{2,1,0:T(8,128)S(1)} %get-tuple-element.40), custom_call_target="InvertDiagBlocksLowerTriangular" | custom-call | tf_op jit(solution)/shard_map/jit(cholesky)/cholesky | solution.py:18
  46.5 0.2 fusion.5
  46.7 0.3 convolution_subtract_fusion.2
  47.0 0.1 copy.26
  47.1 11.7 %cholesky.103 = f32[128,128]{1,0:T(8,128)S(1)} custom-call(f32[128,128]{1,0:T(8,128)S(1)} %convolution_subtract_fusion.2), custom_call_target="Cholesky" | custom-call | tf_op jit(solution)/shard_map/jit(cholesky)/cholesky | solution.py:18
  58.9 0.1 copy.27
  59.0 0.0 copy-start.1
  59.0 0.7 compare_reduce_fusion
  61.0 0.1 triangular_solve.60
  61.1 4.3 %while.1 = (s32[]{:T(128)}, f32[256,256]{0,1:T(8,128)S(1)}, s32[2,2]{1,0:T(2,128)S(1)}, f32[2,128,128]{2,1,0:T(8,128)S(1)}, s32[]{:T(128)}) while((s32[]{:T(128)}, f32[256,256]{0,1:T(8,128)S(1)}, s32[2,2]{1,0:T(2,128)S(1)}, f32[2,128,128]{2,1,0:T(8,128)S(1)}, s32[]{:T(128)}) %tuple.25), condition=%wide.while_cond, body=%wide.while_body.sunk | while | flops 2 | bytes 393329 | solution.py:22
  61.1 0.7 fusion.16
  61.8 1.3 dynamic-slice.7
  63.1 0.1 copy.31
  63.3 0.7 fusion.16
  63.9 1.3 dynamic-slice.7
  65.3 0.1 copy.31
  65.4 19.9 %custom-call.16 = f32[2,128,128]{1,2,0:T(8,128)S(1)} custom-call(f32[2,128,128]{2,1,0:T(8,128)S(1)} %get-tuple-element.12), custom_call_target="InvertDiagBlocksLowerTriangular" | custom-call | tf_op jit(solution)/shard_map/jit(_solve_triangular)/triangular_solve | solution.py:22
  85.3 0.0 copy-done.1
  85.3 0.2 fusion.1
  85.5 0.2 convolution_subtract_fusion.1
  85.8 0.2 fusion.4
  86.0 0.7 maximum_bitcast_fusion
  86.7 0.0 all-gather.2.cloned.1.call-update
  86.7 0.0 all-reduce.3.cloned.1.call-start
  86.8 25.8 %all-gather.2.cloned.1.call-done = f32[1536,256]{1,0:T(8,128)} async-done(((f32[192,256]{1,0:T(8,128)}), f32[1536,256]{1,0:T(8,128)}) %all-gather.2.cloned.1.call-update) | async-done | bytes 1572880 | tf_op jit(solution)/shard_map/all_gather | solution.py:30
  112.6 2.7 %broadcast_select_fusion = f32[1536,256]{1,0:T(8,128)} fusion(f32[1536,256]{1,0:T(8,128)} %all-gather.2.cloned.1.call-done, pred[]{:T(512)S(6)} %eq.6), kind=kLoop, calls=%fused_computation.6 | loop fusion | flops 393216 | bytes 3145729 | tf_op jit(solution)/shard_map/jit(_where)/select_n | solution.py:10
  115.3 0.0 copy-start
  115.3 0.0 all-reduce.3.cloned.1.call-update
  115.3 89.2 %all-reduce.3.cloned.1.call-done = f32[1536,256]{1,0:T(8,128)} async-done(((f32[1536,256]{1,0:T(8,128)}), f32[1536,256]{1,0:T(8,128)}) %all-reduce.3.cloned.1.call-update) | async-done | bytes 1572880 | tf_op jit(solution)/shard_map/psum | solution.py:11
  204.5 0.0 copy-done
  204.5 12.4 %convolution_subtract_fusion = f32[1536,1536]{1,0:T(8,128)} fusion(f32[1536,1536]{1,0:T(8,128)} %param.5, f32[1536,256]{1,0:T(8,128)} %all-reduce.3.cloned.1.call-done, f32[1536,256]{1,0:T(8,128)S(1)} %copy-done), kind=kOutput, calls=%fused_computation.3 | convolution fusion | flops 7250116608 | bytes 22020096 | tf_op jit(solution)/shard_map/dot_general | solution.py:32
  (16 shorter events, 0.3 us)
Async XLA Ops:
  6.5 106.1 %all-gather.2.cloned.1.call-start = ((), (), s32[]{:S(2)}) async-start(), calls=%async_computation | async-start | bytes 1769472 | tf_op jit(solution)/shard_map/all_gather | solution.py:30
  59.0 26.3 %copy-start.1 = (f32[192,256]{1,0:T(8,128)S(1)}, f32[192,256]{1,0:T(8,128)}, u32[]{:S(2)}) copy-start(f32[192,256]{1,0:T(8,128)} %param.4) | copy-start | bytes 589828
  86.7 117.7 %all-reduce.3.cloned.1.call-start = ((), (), s32[]{:S(2)}) async-start(), calls=%async_computation.1 | async-start | bytes 3145728 | tf_op jit(solution)/shard_map/psum | solution.py:11
  115.3 89.2 %copy-start = (f32[1536,256]{1,0:T(8,128)S(1)}, f32[1536,256]{1,0:T(8,128)}, u32[]{:S(2)}) copy-start(f32[1536,256]{1,0:T(8,128)} %all-gather.2.cloned.1.call-done) | copy-start | bytes 4718596
Sparse Core Ops, SparseCore 0:
  86.9 25.7 all-gather.1
  115.9 88.5 all-reduce.2
where the time goes:
time: 224 us
  waiting for transfers between devices  115 us (51%)
  other arithmetic  57.9 us (26%)
  between operations  15.5 us (7%)
  blocking collectives  14.3 us (6%)
  matrix products  13.6 us (6%)
  local copies, waits for them, and re-layouts  7.22 us (3%)
    psum x1, waiting for transfers between devices, from_root(): return lax.psum(block, axis)  89.2 us
    another operation x6, other arithmetic, factor_block(): return jnp.linalg.cholesky(diag_full - shift_value * identity)  34 us
    all_gather x1, waiting for transfers between devices, on_device(): column_panel = lax.all_gather(solved_mine, 'narrow', axis=0, tiled=True)  25.8 us
    another operation x3, other arithmetic, solve_rows(): jax.scipy.linalg.solve_triangular(lower_factor, raw_panel.T, lower=True)  19.9 us
    all_gather x1, blocking collectives, on_device(): diag_full = lax.all_gather(diag_block, 'narrow', axis=0, tiled=True)  14.3 us
    dot_general x1, matrix products, on_device(): lax.dot_general(row_panel, column_panel, (((1,), (1,)), ((), ())), precis...  12.4 us
  transfers between devices with their start and end apart: 2, of which 2 were waited for; matrix products, arithmetic and copies ran while one was open for 0% of the time, Pallas kernels for 0%

commit v1 on v0

--- a/solution.py
+++ b/solution.py
@@ -6,9 +6,15 @@
 unit_gamma = 65538.0 * 2.0 ** (-24) / (1.0 - 65538.0 * 2.0 ** (-24))
 
 
+def gather_and_add(block, axis):
+    pieces = lax.all_gather(block, axis, axis=0, tiled=False)
+    summed = pieces.sum(axis=0)
+    return summed
+
+
 def from_root(block, axis, source):
     block = jnp.where(lax.axis_index(axis) == source, block, jnp.zeros_like(block))
-    return lax.psum(block, axis)
+    return gather_and_add(block, axis)
 
 
 def factor_block(diag_full):

time: 224 us -> 298 us (1.33)
  waiting for transfers between devices: 115 us -> 179 us
  other arithmetic: 57.9 us -> 67.3 us
    all_gather x0 -> x1, waiting for transfers between devices: none -> 154 us  [gather_and_add(): pieces = lax.all_gather(block, axis, axis=0, tiled=False)]
    psum x1 -> x0, waiting for transfers between devices: 89.2 us -> none  [from_root(): return lax.psum(block, axis)]
    reduce_sum x0 -> x1, other arithmetic: none -> 9.39 us  [gather_and_add(): summed = pieces.sum(axis=0)]
where the time goes in v1:
time: 298 us; the launch traced here: 297 us
  waiting for transfers between devices  179 us (60%)
  other arithmetic  67.3 us (23%)
  between operations  15.5 us (5%)
  blocking collectives  14.3 us (5%)
  matrix products  13.1 us (4%)
  local copies, waits for them, and re-layouts  7.22 us (2%)
    all_gather x1, waiting for transfers between devices, gather_and_add(): pieces = lax.all_gather(block, axis, axis=0, tiled=False)  154 us
    another operation x6, other arithmetic, factor_block(): return jnp.linalg.cholesky(diag_full - shift_value * identity)  34 us
    all_gather x1, waiting for transfers between devices, on_device(): column_panel = lax.all_gather(solved_mine, 'narrow', axis=0, tiled=True)  25.8 us
    another operation x3, other arithmetic, solve_rows(): jax.scipy.linalg.solve_triangular(lower_factor, raw_panel.T, lower=True)  19.9 us
    all_gather x1, blocking collectives, on_device(): diag_full = lax.all_gather(diag_block, 'narrow', axis=0, tiled=True)  14.3 us
    dot_general x1, matrix products, on_device(): lax.dot_general(row_panel, column_panel, (((1,), (1,)), ((), ())), precis...  12 us
    reduce_sum x1, other arithmetic, gather_and_add(): summed = pieces.sum(axis=0)  9.39 us
  transfers between devices with their start and end apart: 2, of which 2 were waited for; matrix products, arithmetic and copies ran while one was open for 0% of the time, Pallas kernels for 0%

profile of v1, /device:TPU:0, one launch (start us, length us, event | category | flops | bytes accessed | tf_op | source)
XLA Modules:
  0.0 297.1 jit_solution(754772144670188619)
XLA Ops:
  6.5 0.0 all-gather.4.cloned.1.call-start
  6.6 14.3 %all_gather.12 = f32[256,256]{1,0:T(8,128)S(1)} all-gather(f32[32,256]{1,0:T(8,128)} %param.3), channel_id=1, replica_groups=mesh['wide'=16,'narrow'=8] {'narrow'}, dimensions={0}, use_global_device_ids=true | all-gather | bytes 294912 | tf_op jit(solution)/shard_map/all_gather | solution.py:32
  20.9 0.1 copy.23
  21.0 2.3 gather_fusion
  23.4 0.6 reduce_sum.18
  24.7 0.1 copy.24
  24.9 11.7 %cholesky.49 = f32[128,128]{1,0:T(8,128)S(1)} custom-call(f32[128,128]{1,0:T(8,128)S(1)} %cholesky.115), custom_call_target="Cholesky" | custom-call | tf_op jit(solution)/shard_map/jit(cholesky)/cholesky | solution.py:24
  36.6 0.1 copy.25
  36.7 9.8 %custom-call.15 = f32[1,128,128]{1,2,0:T(8,128)S(1)} custom-call(f32[1,128,128]{2,1,0:T(8,128)S(1)} %get-tuple-element.40), custom_call_target="InvertDiagBlocksLowerTriangular" | custom-call | tf_op jit(solution)/shard_map/jit(cholesky)/cholesky | solution.py:24
  46.5 0.2 fusion.5
  46.7 0.3 convolution_subtract_fusion.2
  47.0 0.1 copy.26
  47.1 11.7 %cholesky.103 = f32[128,128]{1,0:T(8,128)S(1)} custom-call(f32[128,128]{1,0:T(8,128)S(1)} %convolution_subtract_fusion.2), custom_call_target="Cholesky" | custom-call | tf_op jit(solution)/shard_map/jit(cholesky)/cholesky | solution.py:24
  58.9 0.1 copy.27
  59.0 0.0 copy-start.1
  59.0 0.7 compare_reduce_fusion
  61.1 0.1 triangular_solve.60
  61.1 4.3 %while.1 = (s32[]{:T(128)}, f32[256,256]{0,1:T(8,128)S(1)}, s32[2,2]{1,0:T(2,128)S(1)}, f32[2,128,128]{2,1,0:T(8,128)S(1)}, s32[]{:T(128)}) while((s32[]{:T(128)}, f32[256,256]{0,1:T(8,128)S(1)}, s32[2,2]{1,0:T(2,128)S(1)}, f32[2,128,128]{2,1,0:T(8,128)S(1)}, s32[]{:T(128)}) %tuple.25), condition=%wide.while_cond, body=%wide.while_body.sunk | while | flops 2 | bytes 393329 | solution.py:28
  61.1 0.7 fusion.16
  61.8 1.3 dynamic-slice.7
  63.1 0.1 copy.31
  63.3 0.7 fusion.16
  63.9 1.3 dynamic-slice.7
  65.3 0.1 copy.31
  65.4 19.9 %custom-call.16 = f32[2,128,128]{1,2,0:T(8,128)S(1)} custom-call(f32[2,128,128]{2,1,0:T(8,128)S(1)} %get-tuple-element.12), custom_call_target="InvertDiagBlocksLowerTriangular" | custom-call | tf_op jit(solution)/shard_map/jit(_solve_triangular)/triangular_solve | solution.py:28
  85.3 0.0 copy-done.1
  85.3 0.2 fusion.1
  85.5 0.2 convolution_subtract_fusion.1
  85.8 0.2 fusion.4
  86.0 0.7 maximum_bitcast_fusion
  86.7 0.0 all-gather.4.cloned.1.call-update
  86.7 0.0 all-gather.6.cloned.1.call-start
  86.8 25.8 %all-gather.4.cloned.1.call-done = f32[1536,256]{1,0:T(8,128)} async-done(((f32[192,256]{1,0:T(8,128)}), f32[1536,256]{1,0:T(8,128)}) %all-gather.4.cloned.1.call-update) | async-done | bytes 1572880 | tf_op jit(solution)/shard_map/all_gather | solution.py:36
  112.6 2.7 broadcast_select_fusion
  115.3 0.0 all-gather.6.cloned.1.call-update
  115.3 153.6 %all-gather.6.cloned.1.call-done = f32[24576,256]{1,0:T(8,128)} async-done(((f32[1536,256]{1,0:T(8,128)}), f32[24576,256]{1,0:T(8,128)}) %all-gather.6.cloned.1.call-update) | async-done | bytes 25165840 | tf_op jit(solution)/shard_map/all_gather | solution.py:10
  268.9 0.0 copy-start
  268.9 9.4 %reduce_sum.19 = f32[1536,256]{1,0:T(8,128)S(1)} reduce(f32[16,1536,256]{2,1,0:T(8,128)} %bitcast.36, f32[]{:T(128)} %constant.95.clone.1), dimensions={0}, to_apply=%region_5.6 | reduce | flops 5898240 | bytes 26738692 | tf_op jit(solution)/shard_map/reduce_sum | solution.py:11
  278.3 0.0 copy-done
  278.3 12.0 %convolution_subtract_fusion = f32[1536,1536]{1,0:T(8,128)} fusion(f32[1536,1536]{1,0:T(8,128)} %param.5, f32[1536,256]{1,0:T(8,128)S(1)} %reduce_sum.19, f32[1536,256]{1,0:T(8,128)S(1)} %copy-done), kind=kOutput, calls=%fused_computation.3 | convolution fusion | flops 7250116608 | bytes 22020096 | tf_op jit(solution)/shard_map/dot_general | solution.py:38
  (16 shorter events, 0.3 us)
Async XLA Ops:
  6.5 106.1 %all-gather.4.cloned.1.call-start = ((), (), s32[]{:S(2)}) async-start(), calls=%async_computation | async-start | bytes 1769472 | tf_op jit(solution)/shard_map/all_gather | solution.py:36
  59.0 26.3 %copy-start.1 = (f32[192,256]{1,0:T(8,128)S(1)}, f32[192,256]{1,0:T(8,128)}, u32[]{:S(2)}) copy-start(f32[192,256]{1,0:T(8,128)} %param.4) | copy-start | bytes 589828
  86.7 182.2 %all-gather.6.cloned.1.call-start = ((), (), s32[]{:S(2)}) async-start(), calls=%async_computation.1 | async-start | bytes 26738688 | tf_op jit(solution)/shard_map/all_gather | solution.py:10
  268.9 9.4 %copy-start = (f32[1536,256]{1,0:T(8,128)S(1)}, f32[1536,256]{1,0:T(8,128)}, u32[]{:S(2)}) copy-start(f32[1536,256]{1,0:T(8,128)} %all-gather.4.cloned.1.call-done) | copy-start | bytes 4718596
Sparse Core Ops, SparseCore 0:
  86.9 25.7 all-gather.3
  115.4 153.4 all-gather.5
